TPU v7x, 32 devices: a whole 2x2x4 slice. The times are simulated.
32 devices in a mesh: replica: 2 (over y), fsdp: 16 (over z, x, core).
Axes of the slice: x: 2, y: 2, z: 4, core: 2. Of those that a mesh axis runs over, the one named last changes fastest.
Arguments:
- tokens: float32 [6144, 768], P(('replica', 'fsdp')), may hold values from -6 to 6
- segment: int32 [32, 192], P(('replica', 'fsdp')), may hold values from 0 to 7, never falling along the last dimension, each value on 1 to 96 neighbouring positions
- cotangent: float32 [6144, 768], P(('replica', 'fsdp')), may hold values from -6 to 6
- norm1_gain: bfloat16 [768], P('fsdp'), may hold values from 0.5 to 1.5
- norm1_shift: bfloat16 [768], P('fsdp'), may hold values from -1 to 1
- qkv_weight: bfloat16 [768, 2304], P('fsdp'), may hold values from -2 to 2
- qv_bias: bfloat16 [1536], P('fsdp'), may hold values from -1 to 1
- out_weight: bfloat16 [768, 768], P('fsdp'), may hold values from -0.625 to 0.625
- out_bias: bfloat16 [768], P('fsdp'), may hold values from -1 to 1
- norm2_gain: bfloat16 [768], P('fsdp'), may hold values from 0.5 to 1.5
- norm2_shift: bfloat16 [768], P('fsdp'), may hold values from -1 to 1
- fc1_weight: bfloat16 [768, 3072], P('fsdp'), may hold values from -0.109375 to 0.109375
- fc1_bias: bfloat16 [3072], P('fsdp'), may hold values from -1.4 to 1.4
- fc2_weight: bfloat16 [3072, 768], P('fsdp'), may hold values from -0.15625 to 0.15625
- fc2_bias: bfloat16 [768], P('fsdp'), may hold values from -1 to 1
Outputs:
- layer_out: float32 [6144, 768], P(('replica', 'fsdp'))
- grad_tokens: float32 [6144, 768], P(('replica', 'fsdp'))
- grad_norm1_gain: float32 [768], P('fsdp')
- grad_norm1_shift: float32 [768], P('fsdp')
- grad_qkv_weight: float32 [768, 2304], P('fsdp')
- grad_qv_bias: float32 [1536], P('fsdp')
- grad_out_weight: float32 [768, 768], P('fsdp')
- grad_out_bias: float32 [768], P('fsdp')
- grad_norm2_gain: float32 [768], P('fsdp')
- grad_norm2_shift: float32 [768], P('fsdp')
- grad_fc1_weight: float32 [768, 3072], P('fsdp')
- grad_fc1_bias: float32 [3072], P('fsdp')
- grad_fc2_weight: float32 [3072, 768], P('fsdp')
- grad_fc2_bias: float32 [768], P('fsdp')
Inputs may be any that keep to these rules, and one draw needn't show every extreme that they name: `segment`: along each sequence the numbers never fall; a run of equal numbers is one document.
All inputs are finite; a program needn't handle non-finite values.
Results may differ from a plain program's by a relative error of at most 0.025.
The roundings to bfloat16 on the way count: a program that leaves them out, or rounds other values in their place, can miss the bound.
Values may be sent and summed in bfloat16 or wider, within the bound.
No kernel may reach another device: no remote copies, remote signals or barrier semaphores. Data moves between devices by JAX's collectives and lax.ppermute only.
A program may use at most 128 MiB of HBM per device.

v0:
```python
import jax
import jax.numpy as jnp
from jax import lax
from jax.sharding import PartitionSpec as P

D = 768
HEADS = 12
HEAD_DIM = 64
L = 192
EPSILON = 1e-05


def layer_norm(inputs, gain_vec, shift_vec):
    average = jnp.mean(inputs, axis=-1, keepdims=True)
    centered = inputs - average
    variance = jnp.mean(centered * centered, axis=-1, keepdims=True)
    inv_std = lax.rsqrt(variance + EPSILON)
    normed = centered * inv_std
    return (normed * gain_vec.astype(jnp.float32) + shift_vec.astype(jnp.float32), normed, inv_std)


def norm_back(grad_out, normed, inv_std, gain_vec):
    grad_norm = grad_out * gain_vec.astype(jnp.float32)
    first = jnp.mean(grad_norm, axis=-1, keepdims=True)
    second = jnp.mean(grad_norm * normed, axis=-1, keepdims=True)
    grad_in = inv_std * (grad_norm - first - normed * second)
    return (grad_in, jnp.sum(grad_out * normed, axis=0), jnp.sum(grad_out, axis=0))


def allowed_pairs(segment):
    length = segment.shape[1]
    causal = jnp.arange(length)[:, None] >= jnp.arange(length)[None, :]
    same_doc = segment[:, :, None] == segment[:, None, :]
    return (same_doc & causal[None])[:, None]


def masked_scores(queries, key_rows, allowed):
    scores = jnp.einsum(
        "bqhe,bkhe->bhqk", queries, key_rows, preferred_element_type=jnp.float32
    ) * HEAD_DIM ** (-0.5)
    return jnp.where(allowed, scores, -1e30)


def on_device(
    tokens,
    segment,
    cotangent,
    norm1_gain,
    norm1_shift,
    qkv_weight,
    qv_bias,
    out_weight,
    out_bias,
    norm2_gain,
    norm2_shift,
    fc1_weight,
    fc1_bias,
    fc2_weight,
    fc2_bias,
):
    f32 = jnp.float32
    bf16 = jnp.bfloat16
    seq_count = segment.shape[0]
    row_count = tokens.shape[0]
    gathered = (
        lax.all_gather(norm1_gain, "fsdp", axis=0, tiled=True),
        lax.all_gather(norm1_shift, "fsdp", axis=0, tiled=True),
        lax.all_gather(qkv_weight, "fsdp", axis=0, tiled=True),
        lax.all_gather(qv_bias, "fsdp", axis=0, tiled=True),
        lax.all_gather(out_weight, "fsdp", axis=0, tiled=True),
        lax.all_gather(out_bias, "fsdp", axis=0, tiled=True),
        lax.all_gather(norm2_gain, "fsdp", axis=0, tiled=True),
        lax.all_gather(norm2_shift, "fsdp", axis=0, tiled=True),
        lax.all_gather(fc1_weight, "fsdp", axis=0, tiled=True),
        lax.all_gather(fc1_bias, "fsdp", axis=0, tiled=True),
        lax.all_gather(fc2_weight, "fsdp", axis=0, tiled=True),
        lax.all_gather(fc2_bias, "fsdp", axis=0, tiled=True),
    )
    (
        gain_one,
        shift_one,
        qkv_full,
        qv_full,
        out_full,
        out_bias_full,
        gain_two,
        shift_two,
        up_full,
        up_bias_full,
        down_full,
        down_bias_full,
    ) = gathered
    normed1, hat_one, rstd_one = layer_norm(tokens, gain_one, shift_one)
    n_one = normed1.astype(bf16)
    proj = jnp.dot(n_one, qkv_full, preferred_element_type=f32)
    qv_f = qv_full.astype(f32)
    queries = (proj[:, :D] + qv_f[:D]).astype(bf16).reshape(seq_count, L, HEADS, HEAD_DIM)
    key_rows = proj[:, D : 2 * D].astype(bf16).reshape(seq_count, L, HEADS, HEAD_DIM)
    values = (proj[:, 2 * D :] + qv_f[D:]).astype(bf16).reshape(seq_count, L, HEADS, HEAD_DIM)
    allowed = allowed_pairs(segment)
    scores = masked_scores(queries, key_rows, allowed)
    top = jnp.max(scores, axis=-1, keepdims=True)
    log_total = top + jnp.log(jnp.sum(jnp.exp(scores - top), axis=-1, keepdims=True))
    probs_b = jnp.where(allowed, jnp.exp(scores - log_total), 0.0).astype(bf16)
    attn = jnp.einsum("bhqk,bkhe->bqhe", probs_b, values, preferred_element_type=f32)
    attn = attn.reshape(row_count, D).astype(bf16)
    resid = tokens + jnp.dot(attn, out_full, preferred_element_type=f32) + out_bias_full.astype(f32)
    normed2, hat_two, rstd_two = layer_norm(resid, gain_two, shift_two)
    n_two = normed2.astype(bf16)
    pre = jnp.dot(n_two, up_full, preferred_element_type=f32) + up_bias_full.astype(f32)
    act = jnp.maximum(pre, 0.0).astype(bf16)
    layer_out = (
        resid + jnp.dot(act, down_full, preferred_element_type=f32) + down_bias_full.astype(f32)
    )
    again = (
        lax.all_gather(norm1_gain, "fsdp", axis=0, tiled=True),
        lax.all_gather(norm1_shift, "fsdp", axis=0, tiled=True),
        lax.all_gather(qkv_weight, "fsdp", axis=0, tiled=True),
        lax.all_gather(qv_bias, "fsdp", axis=0, tiled=True),
        lax.all_gather(out_weight, "fsdp", axis=0, tiled=True),
        lax.all_gather(out_bias, "fsdp", axis=0, tiled=True),
        lax.all_gather(norm2_gain, "fsdp", axis=0, tiled=True),
        lax.all_gather(norm2_shift, "fsdp", axis=0, tiled=True),
        lax.all_gather(fc1_weight, "fsdp", axis=0, tiled=True),
        lax.all_gather(fc1_bias, "fsdp", axis=0, tiled=True),
        lax.all_gather(fc2_weight, "fsdp", axis=0, tiled=True),
        lax.all_gather(fc2_bias, "fsdp", axis=0, tiled=True),
    )
    (
        gain_one,
        shift_one,
        qkv_full,
        qv_full,
        out_full,
        out_bias_full,
        gain_two,
        shift_two,
        up_full,
        up_bias_full,
        down_full,
        down_bias_full,
    ) = again
    cot_b = cotangent.astype(bf16)
    g_fc2_b = jnp.sum(cotangent, axis=0)
    d_act = jnp.dot(cot_b, down_full.T, preferred_element_type=f32)
    d_pre = jnp.where(pre > 0, d_act, 0.0)
    g_fc1_b = jnp.sum(d_pre, axis=0)
    d_pre_b = d_pre.astype(bf16)
    d_normed2 = jnp.dot(d_pre_b, up_full.T, preferred_element_type=f32)
    d_two, g_gain_two, g_shift_two = norm_back(d_normed2, hat_two, rstd_two, gain_two)
    d_resid = cotangent + d_two
    d_resid_b = d_resid.astype(bf16)
    g_out_b = jnp.sum(d_resid, axis=0)
    d_attn = jnp.dot(d_resid_b, out_full.T, preferred_element_type=f32).astype(bf16)
    d_attn = d_attn.reshape(seq_count, L, HEADS, HEAD_DIM)
    scores = masked_scores(queries, key_rows, allowed)
    probs = jnp.where(allowed, jnp.exp(scores - log_total), 0.0)
    probs_b = probs.astype(bf16)
    d_values = jnp.einsum("bhqk,bqhe->bkhe", probs_b, d_attn, preferred_element_type=f32)
    d_probs = jnp.einsum("bqhe,bkhe->bhqk", d_attn, values, preferred_element_type=f32)
    delta = jnp.sum(probs * d_probs, axis=-1, keepdims=True)
    d_scores = (probs * (d_probs - delta) * HEAD_DIM ** (-0.5)).astype(bf16)
    d_queries = jnp.einsum(
        "bhqk,bkhe->bqhe", d_scores, key_rows, preferred_element_type=f32
    ).reshape(row_count, D)
    d_keys = jnp.einsum("bhqk,bqhe->bkhe", d_scores, queries, preferred_element_type=f32).reshape(
        row_count, D
    )
    d_values = d_values.reshape(row_count, D)
    g_qv_b = jnp.concatenate([jnp.sum(d_queries, axis=0), jnp.sum(d_values, axis=0)])
    d_proj = jnp.concatenate([d_queries, d_keys, d_values], axis=1).astype(bf16)
    d_normed1 = jnp.dot(d_proj, qkv_full.T, preferred_element_type=f32)
    d_one, g_gain_one, g_shift_one = norm_back(d_normed1, hat_one, rstd_one, gain_one)
    grad_tokens = d_resid + d_one
    replicas = lax.axis_size("replica")
    owners = lax.axis_size("fsdp")
    factor = (row_count * replicas * owners) ** (-0.5)
    operand_pairs = ((n_one, d_proj), (attn, d_resid_b), (n_two, d_pre_b), (act, cot_b))
    mats = tuple(
        (
            jnp.dot(left.T, right, preferred_element_type=f32) * factor
            for left, right in operand_pairs
        )
    )
    owned = (
        lax.psum_scatter(g_gain_one * factor, "fsdp", scatter_dimension=0, tiled=True),
        lax.psum_scatter(g_shift_one * factor, "fsdp", scatter_dimension=0, tiled=True),
        lax.psum_scatter(mats[0], "fsdp", scatter_dimension=0, tiled=True),
        lax.psum_scatter(g_qv_b * factor, "fsdp", scatter_dimension=0, tiled=True),
        lax.psum_scatter(mats[1], "fsdp", scatter_dimension=0, tiled=True),
        lax.psum_scatter(g_out_b * factor, "fsdp", scatter_dimension=0, tiled=True),
        lax.psum_scatter(g_gain_two * factor, "fsdp", scatter_dimension=0, tiled=True),
        lax.psum_scatter(g_shift_two * factor, "fsdp", scatter_dimension=0, tiled=True),
        lax.psum_scatter(mats[2], "fsdp", scatter_dimension=0, tiled=True),
        lax.psum_scatter(g_fc1_b * factor, "fsdp", scatter_dimension=0, tiled=True),
        lax.psum_scatter(mats[3], "fsdp", scatter_dimension=0, tiled=True),
        lax.psum_scatter(g_fc2_b * factor, "fsdp", scatter_dimension=0, tiled=True),
    )
    summed = lax.psum(
        (
            owned[0],
            owned[1],
            owned[2],
            owned[3],
            owned[4],
            owned[5],
            owned[6],
            owned[7],
            owned[8],
            owned[9],
            owned[10],
            owned[11],
        ),
        "replica",
    )
    return (layer_out, grad_tokens) + tuple(summed)


def solution(mesh):
    in_specs = (
        P(("replica", "fsdp"), None),
        P(("replica", "fsdp"), None),
        P(("replica", "fsdp"), None),
        P("fsdp"),
        P("fsdp"),
        P("fsdp", None),
        P("fsdp"),
        P("fsdp", None),
        P("fsdp"),
        P("fsdp"),
        P("fsdp"),
        P("fsdp", None),
        P("fsdp"),
        P("fsdp", None),
        P("fsdp"),
    )
    out_specs = (
        P(("replica", "fsdp"), None),
        P(("replica", "fsdp"), None),
        P("fsdp"),
        P("fsdp"),
        P("fsdp", None),
        P("fsdp"),
        P("fsdp", None),
        P("fsdp"),
        P("fsdp"),
        P("fsdp"),
        P("fsdp", None),
        P("fsdp"),
        P("fsdp", None),
        P("fsdp"),
    )
    return jax.shard_map(
        on_device, mesh=mesh, in_specs=in_specs, out_specs=out_specs, check_vma=False
    )
```

profile of v0, /device:TPU:0, one launch (start us, length us, event | category | flops | bytes accessed | tf_op | source)
XLA Modules:
  0.0 705.3 jit_solution(12150744632459119481)
XLA Ops:
  20.0 63.9 %all-reduce.19 = (bf16[768]{0:T(1024)(128)(2,1)S(1)}, bf16[768]{0:T(1024)(128)(2,1)S(1)}, bf16[1536]{0:T(1024)(128)(2,1)S(1)}, bf16[768]{0:T(1024)(128)(2,1)S(1)...) all-reduce(bf16[768]{0:T(1024)(128)(2,1)S(1)} %dynamic-update-slice, ...), channel_id=1, replica_groups=mesh['replica'=2,'fsdp'=16] {'fsdp'}, use_global_device_ids=true, to_apply=%add.1 | all-reduce | flops 9216 | bytes 36864
  88.0 2.9 fusion.42
  94.4 5.4 all-gather.7.cloned.1.call-done
  102.4 51.7 %all-gather.9.cloned.1.call-done = bf16[768,3072]{1,0:T(8,128)(2,1)} async-done(((bf16[48,3072]{1,0:T(8,128)(2,1)}), bf16[768,3072]{1,0:T(8,128)(2,1)}) %all-gather.9.cloned.1.call-update) | async-done | bytes 4718608 | tf_op jit(solution)/shard_map/all_gather | solution.py:74
  154.1 3.5 convolution_add_fusion
  157.6 50.3 %all-gather.11.cloned.1.call-done = bf16[3072,768]{1,0:T(8,128)(2,1)} async-done(((bf16[192,768]{1,0:T(8,128)(2,1)}), bf16[3072,768]{1,0:T(8,128)(2,1)}) %all-gather.11.cloned.1.call-update) | async-done | bytes 4718608 | tf_op jit(solution)/shard_map/all_gather | solution.py:76
  208.0 4.9 fusion.51
  212.9 2.4 multiply_reduce_fusion.1
  219.1 2.8 convolution_convert_fusion.1
  223.8 3.1 fusion.52
  226.9 6.5 fusion.15
  233.4 7.0 fusion.44
  240.4 3.3 fusion.45
  244.4 4.2 convolution_multiply_fusion
  249.3 6.5 convolution_multiply_fusion.2
  255.9 6.2 convolution_multiply_fusion.1
  267.5 5.2 multiply_reduce_fusion.2
  275.1 5.8 reduce-scatter.7.cloned.1.call-done
  280.8 92.9 %reduce-scatter.5.cloned.1.call-done = f32[48,2304]{1,0:T(8,128)} async-done(((f32[768,2304]{1,0:T(8,128)}), f32[48,2304]{1,0:T(8,128)}) %reduce-scatter.5.cloned.1.call-update) | async-done | bytes 442384 | tf_op jit(solution)/shard_map/reduce_scatter | solution.py:188
  373.7 115.0 %reduce-scatter.9.cloned.1.call-done = f32[48,3072]{1,0:T(8,128)} async-done(((f32[768,3072]{1,0:T(8,128)}), f32[48,3072]{1,0:T(8,128)}) %reduce-scatter.9.cloned.1.call-update) | async-done | bytes 589840 | tf_op jit(solution)/shard_map/reduce_scatter | solution.py:194
  488.7 115.0 %reduce-scatter.11.cloned.1.call-done = f32[192,768]{1,0:T(8,128)} async-done(((f32[3072,768]{1,0:T(8,128)}), f32[192,768]{1,0:T(8,128)}) %reduce-scatter.11.cloned.1.call-update) | async-done | bytes 589840 | tf_op jit(solution)/shard_map/reduce_scatter | solution.py:196
  607.5 61.4 %all-reduce.16 = (f32[768]{0:T(1024)}, f32[768]{0:T(1024)}, f32[1536]{0:T(1024)}, f32[768]{0:T(1024)}, f32[768]{0:T(1024)}, /*index=5*/f32[768]{0:T(1024)}, f32[3072]{0:T(1024)}, f32[768]{0:T(1024)}) all-reduce(f32[768]{0:T(1024)} %broadcast_multiply_fusion.6, ...), channel_id=2, replica_groups=mesh['replica'=2,'fsdp'=16] {'fsdp'}, use_global_device_ids=true, to_apply=%region_12.13.clone | all-reduce | flops 9216 | bytes 73728
  679.1 5.7 all-reduce.17
  688.4 4.2 fusion.18
  (149 shorter events, 57.7 us)
Async XLA Ops:
  7.2 80.8 %copy-start = (f32[192,768]{1,0:T(8,128)S(1)}, f32[192,768]{1,0:T(8,128)}, u32[]{:S(2)}) copy-start(f32[192,768]{1,0:T(8,128)} %param.15) | copy-start | bytes 1769476
  7.2 80.7 %all-gather.5.cloned.1.call-start = ((), (), s32[]{:S(2)}) async-start(), calls=%async_computation.4 | async-start | bytes 3760128 | tf_op jit(solution)/shard_map/all_gather | solution.py:68
  7.9 91.9 %all-gather.7.cloned.1.call-start = ((), (), s32[]{:S(2)}) async-start(), calls=%async_computation.5 | async-start | bytes 1253376 | tf_op jit(solution)/shard_map/all_gather | solution.py:70
  8.7 145.4 %all-gather.9.cloned.1.call-start = ((), (), s32[]{:S(2)}) async-start(), calls=%async_computation.6 | async-start | bytes 5013504 | tf_op jit(solution)/shard_map/all_gather | solution.py:74
  9.4 198.5 %all-gather.11.cloned.1.call-start = ((), (), s32[]{:S(2)}) async-start(), calls=%async_computation.7 | async-start | bytes 5013504 | tf_op jit(solution)/shard_map/all_gather | solution.py:76
  10.0 270.8 %reduce-scatter.7.cloned.1.call-start = ((), (), s32[]{:S(2)}) async-start(), calls=%async_computation.9 | async-start | bytes 2506752 | tf_op jit(solution)/shard_map/reduce_scatter | solution.py:190
  85.7 5.2 copy-start.20
  87.9 4.9 copy-start.12
  94.4 8.0 %copy-start.6 = (bf16[12,64,192]{2,1,0:T(8,128)(2,1)}, bf16[12,64,192]{2,1,0:T(8,128)(2,1)S(1)}, u32[]{:S(2)}) copy-start(bf16[12,64,192]{2,1,0:T(8,128)(2,1)S(1)} %convolution_convert_fusion) | copy-start | bytes 884740
  208.0 5.0 copy-start.1
  208.0 5.0 copy-start.17
  208.0 5.0 copy-start.19
  218.9 154.8 %reduce-scatter.5.cloned.1.call-start = ((), (), s32[]{:S(2)}) async-start(), calls=%async_computation.8 | async-start | bytes 7520256 | tf_op jit(solution)/shard_map/reduce_scatter | solution.py:188
  240.4 4.1 copy-start.14
  240.4 4.1 copy-start.21
  240.4 4.1 copy-start.24
  248.7 240.0 %reduce-scatter.9.cloned.1.call-start = ((), (), s32[]{:S(2)}) async-start(), calls=%async_computation.10 | async-start | bytes 10027008 | tf_op jit(solution)/shard_map/reduce_scatter | solution.py:194
  255.8 347.8 %reduce-scatter.11.cloned.1.call-start = ((), (), s32[]{:S(2)}) async-start(), calls=%async_computation.11 | async-start | bytes 10027008 | tf_op jit(solution)/shard_map/reduce_scatter | solution.py:196
  262.0 5.4 copy-start.22
  262.0 5.4 copy-start.25
  262.1 430.5 %all-reduce.22.cloned.1.call-start = ((), (), s32[]{:S(2)}) async-start(), calls=%async_computation.12 | async-start | bytes 3538944 | tf_op jit(solution)/shard_map/psum | solution.py:199
  267.5 6.4 copy-start.27
  267.5 7.0 copy-start.26
  692.6 5.4 copy-start.11
  (14 other events, 24.7 us)
Sparse Core Ops, SparseCore 0:
  10.3 50.2 all-gather.4
  62.9 36.8 all-gather.6
  102.1 51.9 all-gather.8
  156.2 51.6 all-gather.10
  219.0 61.7 reduce-scatter.6
  284.7 88.9 reduce-scatter.4
  377.8 110.8 reduce-scatter.8
  492.8 110.8 reduce-scatter.10
  606.1 55.5 all-reduce.21
where the time goes:
time: 707 us; the launch traced here: 705 us
  waiting for transfers between devices  439 us (62%)
  blocking collectives  131 us (19%)
  matrix products  67.7 us (10%)
  local copies, waits for them, and re-layouts  32.6 us (5%)
  between operations  18.1 us (3%)
  other arithmetic  16.8 us (2%)
    unnamed x2, blocking collectives  125 us
    reduce_scatter x1, waiting for transfers between devices, on_device(): lax.psum_scatter(mats[3], 'fsdp', scatter_dimension=0, tiled=True)  115 us
    reduce_scatter x1, waiting for transfers between devices, on_device(): lax.psum_scatter(mats[2], 'fsdp', scatter_dimension=0, tiled=True)  115 us
    reduce_scatter x1, waiting for transfers between devices, on_device(): lax.psum_scatter(mats[0], 'fsdp', scatter_dimension=0, tiled=True)  92.9 us
    all_gather x1, waiting for transfers between devices, on_device(): lax.all_gather(fc1_weight, 'fsdp', axis=0, tiled=True)  51.7 us
    all_gather x1, waiting for transfers between devices, on_device(): lax.all_gather(fc2_weight, 'fsdp', axis=0, tiled=True)  50.3 us
    unnamed x87, local copies, waits for them, and re-layouts  27.5 us
    dot_general x4, matrix products, on_device(): jnp.dot(left.T, right, preferred_element_type=f32) * factor  18.7 us
  transfers between devices with their start and end apart: 9, of which 7 were waited for; matrix products, arithmetic and copies ran while one was open for 14% of the time, Pallas kernels for 0%

commit v1 on v0

--- a/solution.py
+++ b/solution.py
@@ -8,6 +8,16 @@
 HEAD_DIM = 64
 L = 192
 EPSILON = 1e-05
+
+
+def gather_around(x, axis, dim):
+    ways, here, step = (lax.axis_size(axis), lax.axis_index(axis), x.shape[dim])
+    dims = [n * ways if d == dim else n for d, n in enumerate(x.shape)]
+    full = lax.dynamic_update_slice_in_dim(jnp.zeros(dims, x.dtype), x, here * step, axis=dim)
+    for far in range(1, ways):
+        x = lax.ppermute(x, axis, [(d, (d + 1) % ways) for d in range(ways)])
+        full = lax.dynamic_update_slice_in_dim(full, x, (here - far) % ways * step, axis=dim)
+    return full
 
 
 def layer_norm(inputs, gain_vec, shift_vec):
@@ -73,7 +83,7 @@
         lax.all_gather(norm2_shift, "fsdp", axis=0, tiled=True),
         lax.all_gather(fc1_weight, "fsdp", axis=0, tiled=True),
         lax.all_gather(fc1_bias, "fsdp", axis=0, tiled=True),
-        lax.all_gather(fc2_weight, "fsdp", axis=0, tiled=True),
+        gather_around(fc2_weight, "fsdp", 0),
         lax.all_gather(fc2_bias, "fsdp", axis=0, tiled=True),
     )
     (

time: 707 us -> 719 us (1.017)
  local copies, waits for them, and re-layouts: 32.6 us -> 61.4 us
  waiting for transfers between devices: 439 us -> 421 us
    ppermute x0 -> x15, waiting for transfers between devices: none -> 130 us  [gather_around(): x = lax.ppermute(x, axis, [(d, (d + 1) % ways) for d in range(ways)])]
    reduce_scatter x1, waiting for transfers between devices: 92.9 us -> 0.01 us  [on_device(): lax.psum_scatter(mats[0], 'fsdp', scatter_dimension=0, tiled=True)]
    reduce_scatter x1, waiting for transfers between devices: 115 us -> 68.9 us  [on_device(): lax.psum_scatter(mats[2], 'fsdp', scatter_dimension=0, tiled=True)]
    dynamic_update_slice x0 -> x16, local copies, waits for them, and re-layouts: none -> 18.6 us  [the longest x15 17.9 us: gather_around(): lax.dynamic_update_slice_in_dim(full, x, (here - far) % ways * step, axis...]
    unnamed x87 -> x113, local copies, waits for them, and re-layouts: 27.5 us -> 31.8 us
  transfers between devices with their start and end apart: 9 -> 24, of which waited for: 7 -> 20; matrix products, arithmetic and copies ran while one was open for 14% -> 17% of each run, Pallas kernels for 0% -> 0%
where the time goes in v1:
time: 719 us; the launch traced here: 717 us
  waiting for transfers between devices  421 us (59%)
  blocking collectives  131 us (18%)
  matrix products  68.6 us (10%)
  local copies, waits for them, and re-layouts  61.4 us (9%)
  between operations  18.2 us (3%)
  other arithmetic  16 us (2%)
    ppermute x15, waiting for transfers between devices, gather_around(): x = lax.ppermute(x, axis, [(d, (d + 1) % ways) for d in range(ways)])  130 us
    unnamed x2, blocking collectives  125 us
    reduce_scatter x1, waiting for transfers between devices, on_device(): lax.psum_scatter(mats[3], 'fsdp', scatter_dimension=0, tiled=True)  115 us
    reduce_scatter x1, waiting for transfers between devices, on_device(): lax.psum_scatter(mats[2], 'fsdp', scatter_dimension=0, tiled=True)  68.9 us
    all_gather x1, waiting for transfers between devices, on_device(): lax.all_gather(fc1_weight, 'fsdp', axis=0, tiled=True)  51.7 us
    all_gather x1, waiting for transfers between devices, on_device(): lax.all_gather(fc2_weight, 'fsdp', axis=0, tiled=True)  50.3 us
    unnamed x113, local copies, waits for them, and re-layouts  31.8 us
    dot_general x4, matrix products, on_device(): jnp.dot(left.T, right, preferred_element_type=f32) * factor  18.7 us
  transfers between devices with their start and end apart: 24, of which 20 were waited for; matrix products, arithmetic and copies ran while one was open for 17% of the time, Pallas kernels for 0%

profile of v1, /device:TPU:0, one launch (start us, length us, event | category | flops | bytes accessed | tf_op | source)
XLA Modules:
  0.0 716.9 jit_solution(11355789152999619735)
XLA Ops:
  20.0 63.8 %all-reduce.19 = (bf16[768]{0:T(1024)(128)(2,1)S(1)}, bf16[768]{0:T(1024)(128)(2,1)S(1)}, bf16[1536]{0:T(1024)(128)(2,1)S(1)}, bf16[768]{0:T(1024)(128)(2,1)S(1)...) all-reduce(bf16[768]{0:T(1024)(128)(2,1)S(1)} %dynamic-update-slice, ...), channel_id=1, replica_groups=mesh['replica'=2,'fsdp'=16] {'fsdp'}, use_global_device_ids=true, to_apply=%add.1 | all-reduce | flops 9216 | bytes 36864
  102.7 51.7 %all-gather.9.cloned.1.call-done = bf16[768,3072]{1,0:T(8,128)(2,1)} async-done(((bf16[48,3072]{1,0:T(8,128)(2,1)}), bf16[768,3072]{1,0:T(8,128)(2,1)}) %all-gather.9.cloned.1.call-update) | async-done | bytes 4718608 | tf_op jit(solution)/shard_map/all_gather | solution.py:84
  157.9 50.3 %all-gather.11.cloned.1.call-done = bf16[3072,768]{1,0:T(8,128)(2,1)} async-done(((bf16[192,768]{1,0:T(8,128)(2,1)}), bf16[3072,768]{1,0:T(8,128)(2,1)}) %all-gather.11.cloned.1.call-update) | async-done | bytes 4718608 | tf_op jit(solution)/shard_map/all_gather | solution.py:136
  227.0 7.1 fusion.44
  234.1 6.4 fusion.15
  249.5 6.5 convolution_multiply_fusion.2
  256.0 6.2 convolution_multiply_fusion.1
  262.6 8.9 %collective-permute-done = bf16[192,768]{1,0:T(8,128)(2,1)S(1)} collective-permute-done((bf16[192,768]{1,0:T(8,128)(2,1)}, bf16[192,768]{1,0:T(8,128)(2,1)S(1)}, u32[]{:S(2)}, u32[]{:S(2)}) %collective-permute-start) | collective-permute-done | bytes 294944 | tf_op jit(solution)/shard_map/ppermute | solution.py:18
  272.2 10.0 %collective-permute-done.1 = bf16[192,768]{1,0:T(8,128)(2,1)S(1)} collective-permute-done((bf16[192,768]{1,0:T(8,128)(2,1)S(1)}, bf16[192,768]{1,0:T(8,128)(2,1)S(1)}, u32[]{:S(2)}, u32[]{:S(2)}) %collective-permute-start.1) | collective-permute-done | bytes 294944 | tf_op jit(solution)/shard_map/ppermute | solution.py:18
  282.9 8.1 %collective-permute-done.2 = bf16[192,768]{1,0:T(8,128)(2,1)S(1)} collective-permute-done((bf16[192,768]{1,0:T(8,128)(2,1)S(1)}, bf16[192,768]{1,0:T(8,128)(2,1)S(1)}, u32[]{:S(2)}, u32[]{:S(2)}) %collective-permute-start.2) | collective-permute-done | bytes 294944 | tf_op jit(solution)/shard_map/ppermute | solution.py:18
  291.8 8.8 %collective-permute-done.3 = bf16[192,768]{1,0:T(8,128)(2,1)S(1)} collective-permute-done((bf16[192,768]{1,0:T(8,128)(2,1)S(1)}, bf16[192,768]{1,0:T(8,128)(2,1)S(1)}, u32[]{:S(2)}, u32[]{:S(2)}) %collective-permute-start.3) | collective-permute-done | bytes 294944 | tf_op jit(solution)/shard_map/ppermute | solution.py:18
  300.6 8.8 %collective-permute-done.4 = bf16[192,768]{1,0:T(8,128)(2,1)S(1)} collective-permute-done((bf16[192,768]{1,0:T(8,128)(2,1)S(1)}, bf16[192,768]{1,0:T(8,128)(2,1)S(1)}, u32[]{:S(2)}, u32[]{:S(2)}) %collective-permute-start.4) | collective-permute-done | bytes 294944 | tf_op jit(solution)/shard_map/ppermute | solution.py:18
  310.2 8.2 %collective-permute-done.5 = bf16[192,768]{1,0:T(8,128)(2,1)S(1)} collective-permute-done((bf16[192,768]{1,0:T(8,128)(2,1)S(1)}, bf16[192,768]{1,0:T(8,128)(2,1)S(1)}, u32[]{:S(2)}, u32[]{:S(2)}) %collective-permute-start.5) | collective-permute-done | bytes 294944 | tf_op jit(solution)/shard_map/ppermute | solution.py:18
  319.1 15.3 %collective-permute-done.6 = bf16[192,768]{1,0:T(8,128)(2,1)S(1)} collective-permute-done((bf16[192,768]{1,0:T(8,128)(2,1)S(1)}, bf16[192,768]{1,0:T(8,128)(2,1)S(1)}, u32[]{:S(2)}, u32[]{:S(2)}) %collective-permute-start.6) | collective-permute-done | bytes 294944 | tf_op jit(solution)/shard_map/ppermute | solution.py:18
  335.2 9.5 %collective-permute-done.7 = bf16[192,768]{1,0:T(8,128)(2,1)S(1)} collective-permute-done((bf16[192,768]{1,0:T(8,128)(2,1)S(1)}, bf16[192,768]{1,0:T(8,128)(2,1)S(1)}, u32[]{:S(2)}, u32[]{:S(2)}) %collective-permute-start.7) | collective-permute-done | bytes 294944 | tf_op jit(solution)/shard_map/ppermute | solution.py:18
  345.4 14.4 %collective-permute-done.8 = bf16[192,768]{1,0:T(8,128)(2,1)} collective-permute-done((bf16[192,768]{1,0:T(8,128)(2,1)S(1)}, bf16[192,768]{1,0:T(8,128)(2,1)}, u32[]{:S(2)}, u32[]{:S(2)}) %collective-permute-start.8) | collective-permute-done | bytes 294944 | tf_op jit(solution)/shard_map/ppermute | solution.py:18
  359.9 9.4 %collective-permute-done.9 = bf16[192,768]{1,0:T(8,128)(2,1)} collective-permute-done((bf16[192,768]{1,0:T(8,128)(2,1)}, bf16[192,768]{1,0:T(8,128)(2,1)}, u32[]{:S(2)}, u32[]{:S(2)}) %collective-permute-start.9) | collective-permute-done | bytes 294944 | tf_op jit(solution)/shard_map/ppermute | solution.py:18
  378.1 6.8 collective-permute-done.10
  396.1 6.6 collective-permute-done.12
  413.8 6.7 collective-permute-done.14
  431.4 68.9 %reduce-scatter.9.cloned.1.call-done = f32[48,3072]{1,0:T(8,128)} async-done(((f32[768,3072]{1,0:T(8,128)}), f32[48,3072]{1,0:T(8,128)}) %reduce-scatter.9.cloned.1.call-update) | async-done | bytes 589840 | tf_op jit(solution)/shard_map/reduce_scatter | solution.py:204
  500.3 115.0 %reduce-scatter.11.cloned.1.call-done = f32[192,768]{1,0:T(8,128)} async-done(((f32[3072,768]{1,0:T(8,128)}), f32[192,768]{1,0:T(8,128)}) %reduce-scatter.11.cloned.1.call-update) | async-done | bytes 589840 | tf_op jit(solution)/shard_map/reduce_scatter | solution.py:206
  619.2 61.4 %all-reduce.16 = (f32[768]{0:T(1024)}, f32[768]{0:T(1024)}, f32[1536]{0:T(1024)}, f32[768]{0:T(1024)}, f32[768]{0:T(1024)}, /*index=5*/f32[768]{0:T(1024)}, f32[3072]{0:T(1024)}, f32[768]{0:T(1024)}) all-reduce(f32[768]{0:T(1024)} %broadcast_multiply_fusion.6, ...), channel_id=2, replica_groups=mesh['replica'=2,'fsdp'=16] {'fsdp'}, use_global_device_ids=true, to_apply=%region_12.13.clone | all-reduce | flops 9216 | bytes 73728
  690.8 5.7 all-reduce.17
  (222 shorter events, 134.2 us)
Async XLA Ops:
  7.2 80.7 %all-gather.5.cloned.1.call-start = ((), (), s32[]{:S(2)}) async-start(), calls=%async_computation.4 | async-start | bytes 3760128 | tf_op jit(solution)/shard_map/all_gather | solution.py:78
  7.9 92.1 %all-gather.7.cloned.1.call-start = ((), (), s32[]{:S(2)}) async-start(), calls=%async_computation.5 | async-start | bytes 1253376 | tf_op jit(solution)/shard_map/all_gather | solution.py:80
  8.7 145.7 %all-gather.9.cloned.1.call-start = ((), (), s32[]{:S(2)}) async-start(), calls=%async_computation.6 | async-start | bytes 5013504 | tf_op jit(solution)/shard_map/all_gather | solution.py:84
  9.4 198.8 %all-gather.11.cloned.1.call-start = ((), (), s32[]{:S(2)}) async-start(), calls=%async_computation.7 | async-start | bytes 5013504 | tf_op jit(solution)/shard_map/all_gather | solution.py:136
  10.0 421.4 %reduce-scatter.7.cloned.1.call-start = ((), (), s32[]{:S(2)}) async-start(), calls=%async_computation.9 | async-start | bytes 2506752 | tf_op jit(solution)/shard_map/reduce_scatter | solution.py:200
  219.1 212.3 %reduce-scatter.5.cloned.1.call-start = ((), (), s32[]{:S(2)}) async-start(), calls=%async_computation.8 | async-start | bytes 7520256 | tf_op jit(solution)/shard_map/reduce_scatter | solution.py:198
  248.9 251.4 %reduce-scatter.9.cloned.1.call-start = ((), (), s32[]{:S(2)}) async-start(), calls=%async_computation.10 | async-start | bytes 10027008 | tf_op jit(solution)/shard_map/reduce_scatter | solution.py:204
  256.0 359.3 %reduce-scatter.11.cloned.1.call-start = ((), (), s32[]{:S(2)}) async-start(), calls=%async_computation.11 | async-start | bytes 10027008 | tf_op jit(solution)/shard_map/reduce_scatter | solution.py:206
  262.2 442.0 %all-reduce.22.cloned.1.call-start = ((), (), s32[]{:S(2)}) async-start(), calls=%async_computation.12 | async-start | bytes 3538944 | tf_op jit(solution)/shard_map/psum | solution.py:209
  262.3 9.2 %collective-permute-start = (bf16[192,768]{1,0:T(8,128)(2,1)}, bf16[192,768]{1,0:T(8,128)(2,1)S(1)}, u32[]{:S(2)}, u32[]{:S(2)}) collective-permute-start(bf16[192,768]{1,0:T(8,128)(2,1)} %param.28), channel_id=1, source_target_pairs={{0,1},{1,2},{2,3},{3,4},{4,5},{5,6},{6,7},{7,8},{8,9},{9,10},{10,1... | collective-permute-start | bytes 884744 | tf_op jit(solution)/shard_map/ppermute | solution.py:18
  271.5 10.7 %collective-permute-start.1 = (bf16[192,768]{1,0:T(8,128)(2,1)S(1)}, bf16[192,768]{1,0:T(8,128)(2,1)S(1)}, u32[]{:S(2)}, u32[]{:S(2)}) collective-permute-start(bf16[192,768]{1,0:T(8,128)(2,1)S(1)} %collective-permute-done), channel_id=1, source_target_pairs={{0,1},{1,2},{2,3},{3,4},{4,5},{5,6},{6,7},{7,8},{8,9},{9,10},{10,1... | collective-permute-start | bytes 884744 | tf_op jit(solution)/shard_map/ppermute | solution.py:18
  282.2 8.8 %collective-permute-start.2 = (bf16[192,768]{1,0:T(8,128)(2,1)S(1)}, bf16[192,768]{1,0:T(8,128)(2,1)S(1)}, u32[]{:S(2)}, u32[]{:S(2)}) collective-permute-start(bf16[192,768]{1,0:T(8,128)(2,1)S(1)} %collective-permute-done.1), channel_id=1, source_target_pairs={{0,1},{1,2},{2,3},{3,4},{4,5},{5,6},{6,7},{7,8},{8,9},{9,10},{10,1... | collective-permute-start | bytes 884744 | tf_op jit(solution)/shard_map/ppermute | solution.py:18
  291.8 8.8 %collective-permute-start.3 = (bf16[192,768]{1,0:T(8,128)(2,1)S(1)}, bf16[192,768]{1,0:T(8,128)(2,1)S(1)}, u32[]{:S(2)}, u32[]{:S(2)}) collective-permute-start(bf16[192,768]{1,0:T(8,128)(2,1)S(1)} %collective-permute-done.2), channel_id=1, source_target_pairs={{0,1},{1,2},{2,3},{3,4},{4,5},{5,6},{6,7},{7,8},{8,9},{9,10},{10,1... | collective-permute-start | bytes 884744 | tf_op jit(solution)/shard_map/ppermute | solution.py:18
  300.6 8.8 %collective-permute-start.4 = (bf16[192,768]{1,0:T(8,128)(2,1)S(1)}, bf16[192,768]{1,0:T(8,128)(2,1)S(1)}, u32[]{:S(2)}, u32[]{:S(2)}) collective-permute-start(bf16[192,768]{1,0:T(8,128)(2,1)S(1)} %collective-permute-done.3), channel_id=1, source_target_pairs={{0,1},{1,2},{2,3},{3,4},{4,5},{5,6},{6,7},{7,8},{8,9},{9,10},{10,1... | collective-permute-start | bytes 884744 | tf_op jit(solution)/shard_map/ppermute | solution.py:18
  309.5 8.9 %collective-permute-start.5 = (bf16[192,768]{1,0:T(8,128)(2,1)S(1)}, bf16[192,768]{1,0:T(8,128)(2,1)S(1)}, u32[]{:S(2)}, u32[]{:S(2)}) collective-permute-start(bf16[192,768]{1,0:T(8,128)(2,1)S(1)} %collective-permute-done.4), channel_id=1, source_target_pairs={{0,1},{1,2},{2,3},{3,4},{4,5},{5,6},{6,7},{7,8},{8,9},{9,10},{10,1... | collective-permute-start | bytes 884744 | tf_op jit(solution)/shard_map/ppermute | solution.py:18
  319.1 15.3 %collective-permute-start.6 = (bf16[192,768]{1,0:T(8,128)(2,1)S(1)}, bf16[192,768]{1,0:T(8,128)(2,1)S(1)}, u32[]{:S(2)}, u32[]{:S(2)}) collective-permute-start(bf16[192,768]{1,0:T(8,128)(2,1)S(1)} %collective-permute-done.5), channel_id=1, source_target_pairs={{0,1},{1,2},{2,3},{3,4},{4,5},{5,6},{6,7},{7,8},{8,9},{9,10},{10,1... | collective-permute-start | bytes 884744 | tf_op jit(solution)/shard_map/ppermute | solution.py:18
  334.4 10.2 %collective-permute-start.7 = (bf16[192,768]{1,0:T(8,128)(2,1)S(1)}, bf16[192,768]{1,0:T(8,128)(2,1)S(1)}, u32[]{:S(2)}, u32[]{:S(2)}) collective-permute-start(bf16[192,768]{1,0:T(8,128)(2,1)S(1)} %collective-permute-done.6), channel_id=1, source_target_pairs={{0,1},{1,2},{2,3},{3,4},{4,5},{5,6},{6,7},{7,8},{8,9},{9,10},{10,1... | collective-permute-start | bytes 884744 | tf_op jit(solution)/shard_map/ppermute | solution.py:18
  345.4 14.4 %collective-permute-start.8 = (bf16[192,768]{1,0:T(8,128)(2,1)S(1)}, bf16[192,768]{1,0:T(8,128)(2,1)}, u32[]{:S(2)}, u32[]{:S(2)}) collective-permute-start(bf16[192,768]{1,0:T(8,128)(2,1)S(1)} %collective-permute-done.7), channel_id=1, source_target_pairs={{0,1},{1,2},{2,3},{3,4},{4,5},{5,6},{6,7},{7,8},{8,9},{9,10},{10,1... | collective-permute-start | bytes 884744 | tf_op jit(solution)/shard_map/ppermute | solution.py:18
  359.8 9.4 %collective-permute-start.9 = (bf16[192,768]{1,0:T(8,128)(2,1)}, bf16[192,768]{1,0:T(8,128)(2,1)}, u32[]{:S(2)}, u32[]{:S(2)}) collective-permute-start(bf16[192,768]{1,0:T(8,128)(2,1)} %collective-permute-done.8), channel_id=1, source_target_pairs={{0,1},{1,2},{2,3},{3,4},{4,5},{5,6},{6,7},{7,8},{8,9},{9,10},{10,1... | collective-permute-start | bytes 884744 | tf_op jit(solution)/shard_map/ppermute | solution.py:18
  369.2 15.6 %collective-permute-start.10 = (bf16[192,768]{1,0:T(8,128)(2,1)}, bf16[192,768]{1,0:T(8,128)(2,1)}, u32[]{:S(2)}, u32[]{:S(2)}) collective-permute-start(bf16[192,768]{1,0:T(8,128)(2,1)} %collective-permute-done.9), channel_id=1, source_target_pairs={{0,1},{1,2},{2,3},{3,4},{4,5},{5,6},{6,7},{7,8},{8,9},{9,10},{10,1... | collective-permute-start | bytes 884744 | tf_op jit(solution)/shard_map/ppermute | solution.py:18
  384.8 9.1 %collective-permute-start.11 = (bf16[192,768]{1,0:T(8,128)(2,1)}, bf16[192,768]{1,0:T(8,128)(2,1)S(1)}, u32[]{:S(2)}, u32[]{:S(2)}) collective-permute-start(bf16[192,768]{1,0:T(8,128)(2,1)} %collective-permute-done.10), channel_id=1, source_target_pairs={{0,1},{1,2},{2,3},{3,4},{4,5},{5,6},{6,7},{7,8},{8,9},{9,10},{10,1... | collective-permute-start | bytes 884744 | tf_op jit(solution)/shard_map/ppermute | solution.py:18
  393.9 8.8 %collective-permute-start.12 = (bf16[192,768]{1,0:T(8,128)(2,1)S(1)}, bf16[192,768]{1,0:T(8,128)(2,1)S(1)}, u32[]{:S(2)}, u32[]{:S(2)}) collective-permute-start(bf16[192,768]{1,0:T(8,128)(2,1)S(1)} %collective-permute-done.11), channel_id=1, source_target_pairs={{0,1},{1,2},{2,3},{3,4},{4,5},{5,6},{6,7},{7,8},{8,9},{9,10},{10,1... | collective-permute-start | bytes 884744 | tf_op jit(solution)/shard_map/ppermute | solution.py:18
  402.7 8.8 %collective-permute-start.13 = (bf16[192,768]{1,0:T(8,128)(2,1)S(1)}, bf16[192,768]{1,0:T(8,128)(2,1)S(1)}, u32[]{:S(2)}, u32[]{:S(2)}) collective-permute-start(bf16[192,768]{1,0:T(8,128)(2,1)S(1)} %collective-permute-done.12), channel_id=1, source_target_pairs={{0,1},{1,2},{2,3},{3,4},{4,5},{5,6},{6,7},{7,8},{8,9},{9,10},{10,1... | collective-permute-start | bytes 884744 | tf_op jit(solution)/shard_map/ppermute | solution.py:18
  411.6 8.8 %collective-permute-start.14 = (bf16[192,768]{1,0:T(8,128)(2,1)S(1)}, bf16[192,768]{1,0:T(8,128)(2,1)S(1)}, u32[]{:S(2)}, u32[]{:S(2)}) collective-permute-start(bf16[192,768]{1,0:T(8,128)(2,1)S(1)} %collective-permute-done.13), channel_id=1, source_target_pairs={{0,1},{1,2},{2,3},{3,4},{4,5},{5,6},{6,7},{7,8},{8,9},{9,10},{10,1... | collective-permute-start | bytes 884744 | tf_op jit(solution)/shard_map/ppermute | solution.py:18
  (42 other events, 368.9 us)
Sparse Core Ops, SparseCore 0:
  10.3 50.5 all-gather.4
  63.1 36.8 all-gather.6
  102.3 51.9 all-gather.8
  156.5 51.6 all-gather.10
  219.3 61.8 reduce-scatter.6
  285.0 97.4 reduce-scatter.4
  386.6 113.5 reduce-scatter.8
  504.4 110.8 reduce-scatter.10
  617.8 55.5 all-reduce.21
